TPU v7x, 32 devices: a whole 2x2x4 slice. The times are simulated.
32 devices in a mesh: layer: 8 (over z, x), tile: 4 (over y, core).
Axes of the slice: x: 2, y: 2, z: 4, core: 2. Of those that a mesh axis runs over, the one named last changes fastest.
Arguments:
- source_modes: bfloat16 [8, 8, 2, 32, 512], P('layer', None, None, 'tile'), may hold values from -6 to 6
- port_cells: int32 [8], replicated, may hold values from 0 to 511
- frequencies: float32 [2], replicated, may hold values from 0.3 to 1.5, as said below
- layer_inverse: bfloat16 [8, 2, 32, 512, 512], P('layer', None, 'tile'), may hold values from -0.092807765 to 1.6928078
- coupling_self: float32 [8, 2, 32, 512], P('layer', None, 'tile'), may hold values from 0.4 to 1
- coupling_curl: float32 [8, 2, 32, 512], P('layer', None, 'tile'), may hold values from -4 to 4
Outputs:
- snapshot_basis: float32 [8, 32, 2, 32, 512], P('layer', None, None, 'tile')
- triangle: float32 [32, 32], replicated
Inputs may be any that keep to these rules, and one draw needn't show every extreme that they name: `port_cells`: each port's profile is centred on this plane column. `frequencies`: the second frequency is 1.5 to 2.5 times the first.
All inputs are finite; a program needn't handle non-finite values.
Results may differ from a plain program's by a relative error of at most 0.04.
Values may be sent and summed in bfloat16 or wider, within the bound.
A program may use at most 64 MiB of HBM per device.

v0:
```python
import jax
import jax.numpy as jnp
from jax import lax
from jax.sharding import PartitionSpec as P


def with_halo(cells, sides, width):
    for axis, dim in sides:
        count = lax.axis_size(axis)
        ends = count - 1
        head = lax.slice_in_dim(cells, 0, width, axis=dim)
        tail = lax.slice_in_dim(cells, cells.shape[dim] - width, cells.shape[dim], axis=dim)
        cells = jnp.concatenate(
            [
                lax.ppermute(tail, axis, [(i, (i + 1) % count) for i in range(ends)]),
                cells,
                lax.ppermute(head, axis, [((i + 1) % count, i) for i in range(ends)]),
            ],
            axis=dim,
        )
    return cells


def shifted(array, axis, by):
    size = lax.axis_size(axis)
    pairs = [(i, i + by) for i in range(size) if 0 <= i + by < size]
    return lax.ppermute(array, axis, pairs)


def lower_factor(gram):
    order = gram.shape[0]
    index_row = jnp.arange(order)

    def column_step(col_no, lower):
        unit = (index_row == col_no).astype(gram.dtype)
        column = jnp.dot(gram, unit, precision=lax.Precision.HIGHEST)
        lower_row = jnp.dot(unit, lower, precision=lax.Precision.HIGHEST)
        column = column - jnp.dot(lower, lower_row, precision=lax.Precision.HIGHEST)
        pivot = jnp.sqrt(jnp.sum(column * unit))
        scaled = jnp.where(index_row >= col_no, column / pivot, 0.0)
        return lower + scaled[:, None] * unit[None, :]

    return lax.fori_loop(0, order, column_step, jnp.zeros_like(gram))


def lower_inverse(lower):
    order = lower.shape[0]
    index_row = jnp.arange(order)

    def row_step(row_no, inverse):
        unit = (index_row == row_no).astype(lower.dtype)
        lower_row = jnp.dot(unit, lower, precision=lax.Precision.HIGHEST)
        pivot = jnp.sum(lower_row * unit)
        new_row = (unit - jnp.dot(lower_row, inverse, precision=lax.Precision.HIGHEST)) / pivot
        return inverse + unit[:, None] * new_row[None, :]

    return lax.fori_loop(0, order, row_step, jnp.zeros_like(lower))


def per_device(source_modes, port_cells, frequencies, layer_inverse, coupling_self, coupling_curl):
    layers_total = lax.axis_size("layer")
    tile_count = lax.axis_size("tile")
    layer_pos = lax.axis_index("layer")
    inverse_block = layer_inverse[0]
    self_w = coupling_self[0]
    curl_w = coupling_curl[0]
    rows_dev = source_modes.shape[3]
    plane_width = source_modes.shape[4]
    columns = jnp.arange(plane_width, dtype=jnp.float32)
    offsets = (columns[None, :] - port_cells.astype(jnp.float32)[:, None]) / (plane_width // 8)
    port_taper = 1.0 / (1.0 + offsets * offsets)
    phase_angle = frequencies * (layer_pos + 1).astype(jnp.float32)
    phase_pair = jnp.stack([jnp.cos(phase_angle), jnp.sin(phase_angle)], axis=1)
    source_layer = source_modes[0].astype(jnp.float32)
    forcing = (
        source_layer[:, None, None]
        * port_taper[:, None, None, None, None, :]
        * phase_pair[None, :, :, None, None, None]
    )
    forcing = forcing.reshape((-1, 2, rows_dev, plane_width))
    column_total = forcing.shape[0]
    group_count = 4
    group_width = column_total // group_count
    forcing_groups = forcing.reshape(group_count, group_width, 2, rows_dev, plane_width)
    step_count = layers_total + group_count - 1

    def couple(field):
        x_part = field[:, 0].astype(jnp.float32)
        y_part = field[:, 1].astype(jnp.float32)
        rim_rows = with_halo(y_part, (("tile", 1),), 1)
        row_diff = rim_rows[:, 2:] - rim_rows[:, :-2]
        cols_pad = jnp.pad(x_part, ((0, 0), (0, 0), (1, 1)))
        col_diff = cols_pad[:, :, 2:] - cols_pad[:, :, :-2]
        part_one = self_w[0] * x_part + curl_w[0] * row_diff
        part_two = self_w[1] * y_part + curl_w[1] * col_diff
        return jnp.stack([part_one, part_two], axis=1)

    def apply_inverse(vectors):
        return jnp.einsum(
            "crik,jcrk->jcri", inverse_block, vectors, preferred_element_type=jnp.float32
        )

    store_shape = (group_count, group_width, 2, rows_dev, plane_width)
    group_shape = (group_width, 2, rows_dev, plane_width)

    def down_step(step_no, state_pair):
        stored, incoming = state_pair
        group_no = jnp.clip(step_no - layer_pos, 0, group_count - 1)
        forcing_now = lax.dynamic_index_in_dim(forcing_groups, group_no, 0, keepdims=False)
        residue = (forcing_now - couple(incoming)).astype(jnp.bfloat16)
        current = apply_inverse(residue).astype(jnp.bfloat16)
        stored = lax.dynamic_update_index_in_dim(stored, current, group_no, 0)
        incoming = shifted(current, "layer", 1)
        return (stored, incoming)

    down_store, _ = lax.fori_loop(
        0,
        step_count,
        down_step,
        (jnp.zeros(store_shape, jnp.bfloat16), jnp.zeros(group_shape, jnp.bfloat16)),
    )
    reverse_pos = layers_total - 1 - layer_pos

    def up_step(step_no, state_pair):
        stored, incoming = state_pair
        group_no = jnp.clip(step_no - reverse_pos, 0, group_count - 1)
        earlier = lax.dynamic_index_in_dim(down_store, group_no, 0, keepdims=False)
        up_image = couple(incoming).astype(jnp.bfloat16)
        current = earlier.astype(jnp.float32) - apply_inverse(up_image)
        stored = lax.dynamic_update_index_in_dim(stored, current, group_no, 0)
        incoming = shifted(current, "layer", -1)
        return (stored, incoming)

    up_store, _ = lax.fori_loop(
        0,
        step_count,
        up_step,
        (jnp.zeros(store_shape, jnp.float32), jnp.zeros(group_shape, jnp.float32)),
    )
    columns_mat = up_store.reshape(column_total, -1)
    gram_local = jnp.dot(columns_mat, columns_mat.T, precision=lax.Precision.HIGHEST)
    total_rows = layers_total * tile_count * columns_mat.shape[1]
    gram_whole = lax.psum(gram_local, ("layer", "tile"))
    triangle = lower_factor(gram_whole / total_rows).T
    solved = jnp.dot(lower_inverse(triangle.T), columns_mat, precision=lax.Precision.HIGHEST)
    basis_out = solved.reshape(1, column_total, 2, rows_dev, plane_width)
    return (basis_out, triangle)


def solution(mesh):
    in_specs = (
        P("layer", None, None, "tile", None),
        P(),
        P(),
        P("layer", None, "tile", None, None),
        P("layer", None, "tile", None),
        P("layer", None, "tile", None),
    )
    out_specs = (P("layer", None, None, "tile", None), P())
    return jax.shard_map(
        per_device, mesh=mesh, in_specs=in_specs, out_specs=out_specs, check_vma=False
    )
```

profile of v0, /device:TPU:0, one launch (start us, length us, event | category | flops | bytes accessed | tf_op | source)
XLA Modules:
  0.0 634.1 jit_solution(17380595981949021285)
XLA Ops:
  3.6 223.6 %while.63 = (s32[]{:T(128)}, bf16[4,8,2,8,512]{4,1,3,2,0:T(8,128)(2,1)S(1)}, bf16[8,2,8,512]{3,0,2,1:T(8,128)(2,1)S(1)}, s32[]{:T(128)}, f32[4,8,2,8,512]{4,3,2,...) while((s32[]{:T(128)}, ...), condition=%wide.region_1.2_spmd, body=%wide.region_0.1_spmd.sunk | while | flops 67829760 | bytes 11698449 | solution.py:116
  11.4 5.7 bitcast_dynamic-update-slice_fusion.4
  30.1 5.7 bitcast_dynamic-update-slice_fusion.4
  49.8 5.7 bitcast_dynamic-update-slice_fusion.4
  69.5 5.7 bitcast_dynamic-update-slice_fusion.4
  110.7 5.7 bitcast_dynamic-update-slice_fusion.4
  131.3 5.7 bitcast_dynamic-update-slice_fusion.4
  172.5 5.7 bitcast_dynamic-update-slice_fusion.4
  193.1 5.7 bitcast_dynamic-update-slice_fusion.4
  227.3 250.6 %while.64 = (s32[]{:T(128)}, f32[4,8,2,8,512]{4,1,3,2,0:T(8,128)S(1)}, f32[8,2,8,512]{3,0,2,1:T(8,128)S(1)}, s32[]{:T(128)}, bf16[4,8,2,8,512]{4,1,3,2,0:T(8,128...) while((s32[]{:T(128)}, ...), condition=%wide.region_3.4_spmd, body=%wide.region_2.3_spmd.sunk | while | flops 67698688 | bytes 11829517 | solution.py:134
  241.4 9.3 %collective-permute-done.5 = f32[8,2,8,512]{3,0,2,1:T(8,128)S(1)} collective-permute-done((f32[8,2,8,512]{3,0,2,1:T(8,128)S(1)}, f32[8,2,8,512]{3,0,2,1:T(8,128)S(1)}, u32[]{:S(2)}, u32[]{:S(2)}) %collective-permute-start.5) | collective-permute-done | bytes 262176 | tf_op jit(solution)/shard_map/while/body/eval_jaxpr/ppermute | solution.py:27
  264.5 9.6 %collective-permute-done.5 = f32[8,2,8,512]{3,0,2,1:T(8,128)S(1)} collective-permute-done((f32[8,2,8,512]{3,0,2,1:T(8,128)S(1)}, f32[8,2,8,512]{3,0,2,1:T(8,128)S(1)}, u32[]{:S(2)}, u32[]{:S(2)}) %collective-permute-start.5) | collective-permute-done | bytes 262176 | tf_op jit(solution)/shard_map/while/body/eval_jaxpr/ppermute | solution.py:27
  287.6 9.4 %collective-permute-done.5 = f32[8,2,8,512]{3,0,2,1:T(8,128)S(1)} collective-permute-done((f32[8,2,8,512]{3,0,2,1:T(8,128)S(1)}, f32[8,2,8,512]{3,0,2,1:T(8,128)S(1)}, u32[]{:S(2)}, u32[]{:S(2)}) %collective-permute-start.5) | collective-permute-done | bytes 262176 | tf_op jit(solution)/shard_map/while/body/eval_jaxpr/ppermute | solution.py:27
  310.2 9.4 %collective-permute-done.5 = f32[8,2,8,512]{3,0,2,1:T(8,128)S(1)} collective-permute-done((f32[8,2,8,512]{3,0,2,1:T(8,128)S(1)}, f32[8,2,8,512]{3,0,2,1:T(8,128)S(1)}, u32[]{:S(2)}, u32[]{:S(2)}) %collective-permute-start.5) | collective-permute-done | bytes 262176 | tf_op jit(solution)/shard_map/while/body/eval_jaxpr/ppermute | solution.py:27
  332.8 9.4 %collective-permute-done.5 = f32[8,2,8,512]{3,0,2,1:T(8,128)S(1)} collective-permute-done((f32[8,2,8,512]{3,0,2,1:T(8,128)S(1)}, f32[8,2,8,512]{3,0,2,1:T(8,128)S(1)}, u32[]{:S(2)}, u32[]{:S(2)}) %collective-permute-start.5) | collective-permute-done | bytes 262176 | tf_op jit(solution)/shard_map/while/body/eval_jaxpr/ppermute | solution.py:27
  355.4 9.4 %collective-permute-done.5 = f32[8,2,8,512]{3,0,2,1:T(8,128)S(1)} collective-permute-done((f32[8,2,8,512]{3,0,2,1:T(8,128)S(1)}, f32[8,2,8,512]{3,0,2,1:T(8,128)S(1)}, u32[]{:S(2)}, u32[]{:S(2)}) %collective-permute-start.5) | collective-permute-done | bytes 262176 | tf_op jit(solution)/shard_map/while/body/eval_jaxpr/ppermute | solution.py:27
  378.1 9.4 %collective-permute-done.5 = f32[8,2,8,512]{3,0,2,1:T(8,128)S(1)} collective-permute-done((f32[8,2,8,512]{3,0,2,1:T(8,128)S(1)}, f32[8,2,8,512]{3,0,2,1:T(8,128)S(1)}, u32[]{:S(2)}, u32[]{:S(2)}) %collective-permute-start.5) | collective-permute-done | bytes 262176 | tf_op jit(solution)/shard_map/while/body/eval_jaxpr/ppermute | solution.py:27
  400.7 9.4 %collective-permute-done.5 = f32[8,2,8,512]{3,0,2,1:T(8,128)S(1)} collective-permute-done((f32[8,2,8,512]{3,0,2,1:T(8,128)S(1)}, f32[8,2,8,512]{3,0,2,1:T(8,128)S(1)}, u32[]{:S(2)}, u32[]{:S(2)}) %collective-permute-start.5) | collective-permute-done | bytes 262176 | tf_op jit(solution)/shard_map/while/body/eval_jaxpr/ppermute | solution.py:27
  423.3 9.4 %collective-permute-done.5 = f32[8,2,8,512]{3,0,2,1:T(8,128)S(1)} collective-permute-done((f32[8,2,8,512]{3,0,2,1:T(8,128)S(1)}, f32[8,2,8,512]{3,0,2,1:T(8,128)S(1)}, u32[]{:S(2)}, u32[]{:S(2)}) %collective-permute-start.5) | collective-permute-done | bytes 262176 | tf_op jit(solution)/shard_map/while/body/eval_jaxpr/ppermute | solution.py:27
  445.9 9.4 %collective-permute-done.5 = f32[8,2,8,512]{3,0,2,1:T(8,128)S(1)} collective-permute-done((f32[8,2,8,512]{3,0,2,1:T(8,128)S(1)}, f32[8,2,8,512]{3,0,2,1:T(8,128)S(1)}, u32[]{:S(2)}, u32[]{:S(2)}) %collective-permute-start.5) | collective-permute-done | bytes 262176 | tf_op jit(solution)/shard_map/while/body/eval_jaxpr/ppermute | solution.py:27
  468.6 9.4 %collective-permute-done.5 = f32[8,2,8,512]{3,0,2,1:T(8,128)S(1)} collective-permute-done((f32[8,2,8,512]{3,0,2,1:T(8,128)S(1)}, f32[8,2,8,512]{3,0,2,1:T(8,128)S(1)}, u32[]{:S(2)}, u32[]{:S(2)}) %collective-permute-start.5) | collective-permute-done | bytes 262176 | tf_op jit(solution)/shard_map/while/body/eval_jaxpr/ppermute | solution.py:27
  478.9 41.6 %psum.7 = f32[32,32]{1,0:T(8,128)S(1)} all-reduce(f32[32,32]{1,0:T(8,128)S(1)} %fusion.62), channel_id=1, replica_groups=mesh['layer'=8,'tile'=4] {'layer','tile'}, use_global_device_ids=true, to_apply=%region_4.5 | all-reduce | flops 1024 | bytes 8192 | tf_op jit(solution)/shard_map/psum | solution.py:143
  520.5 58.2 %while.66 = (s32[]{:T(128)}, f32[32,32]{1,0:T(8,128)S(1)}, f32[32,32]{1,0:T(8,128)S(1)}, s32[]{:T(128)}, s32[]{:T(128)}) while((s32[]{:T(128)}, f32[32,32]{1,0:T(8,128)S(1)}, f32[32,32]{1,0:T(8,128)S(1)}, s32[]{:T(128)}, s32[]{:T(128)}) %tuple.180), condition=%wide.region_7.8_spmd.clone.clone, body=%wide.region_5.7_spmd.clone.clone.sunk | while | flops 42338 | bytes 21869 | solution.py:43
  578.7 50.9 %while.65 = (s32[]{:T(128)}, f32[32,32]{1,0:T(8,128)S(1)}, f32[32,32]{1,0:T(8,128)S(1)}, s32[]{:T(128)}, s32[]{:T(128)}) while((s32[]{:T(128)}, f32[32,32]{1,0:T(8,128)S(1)}, f32[32,32]{1,0:T(8,128)S(1)}, s32[]{:T(128)}, s32[]{:T(128)}) %tuple.183), condition=%wide.region_10.11_spmd.clone, body=%wide.region_8.10_spmd.clone.sunk | while | flops 28994 | bytes 17244 | solution.py:57
  (576 shorter events, 419.4 us)
Async XLA Ops:
  17.0 5.9 collective-permute-start.2
  35.8 6.9 %collective-permute-start.2 = (bf16[8,2,8,512]{3,0,2,1:T(8,128)(2,1)S(1)}, bf16[8,2,8,512]{3,0,2,1:T(8,128)(2,1)S(1)}, u32[]{:S(2)}, u32[]{:S(2)}) collective-permute-start(bf16[8,2,8,512]{3,0,2,1:T(8,128)(2,1)S(1)} %bitcast.184), channel_id=1, source_target_pairs={{0,4},{4,8},{8,12},{12,16},{16,20},{20,24},{24,28},{1,5},{5,9},{9,... | collective-permute-start | bytes 393224 | tf_op jit(solution)/shard_map/while/body/eval_jaxpr/ppermute | solution.py:27
  55.5 6.9 %collective-permute-start.2 = (bf16[8,2,8,512]{3,0,2,1:T(8,128)(2,1)S(1)}, bf16[8,2,8,512]{3,0,2,1:T(8,128)(2,1)S(1)}, u32[]{:S(2)}, u32[]{:S(2)}) collective-permute-start(bf16[8,2,8,512]{3,0,2,1:T(8,128)(2,1)S(1)} %bitcast.184), channel_id=1, source_target_pairs={{0,4},{4,8},{8,12},{12,16},{16,20},{20,24},{24,28},{1,5},{5,9},{9,... | collective-permute-start | bytes 393224 | tf_op jit(solution)/shard_map/while/body/eval_jaxpr/ppermute | solution.py:27
  75.2 7.8 %collective-permute-start.2 = (bf16[8,2,8,512]{3,0,2,1:T(8,128)(2,1)S(1)}, bf16[8,2,8,512]{3,0,2,1:T(8,128)(2,1)S(1)}, u32[]{:S(2)}, u32[]{:S(2)}) collective-permute-start(bf16[8,2,8,512]{3,0,2,1:T(8,128)(2,1)S(1)} %bitcast.184), channel_id=1, source_target_pairs={{0,4},{4,8},{8,12},{12,16},{16,20},{20,24},{24,28},{1,5},{5,9},{9,... | collective-permute-start | bytes 393224 | tf_op jit(solution)/shard_map/while/body/eval_jaxpr/ppermute | solution.py:27
  83.0 5.6 collective-permute-start
  95.8 7.8 %collective-permute-start.2 = (bf16[8,2,8,512]{3,0,2,1:T(8,128)(2,1)S(1)}, bf16[8,2,8,512]{3,0,2,1:T(8,128)(2,1)S(1)}, u32[]{:S(2)}, u32[]{:S(2)}) collective-permute-start(bf16[8,2,8,512]{3,0,2,1:T(8,128)(2,1)S(1)} %bitcast.184), channel_id=1, source_target_pairs={{0,4},{4,8},{8,12},{12,16},{16,20},{20,24},{24,28},{1,5},{5,9},{9,... | collective-permute-start | bytes 393224 | tf_op jit(solution)/shard_map/while/body/eval_jaxpr/ppermute | solution.py:27
  116.4 7.8 %collective-permute-start.2 = (bf16[8,2,8,512]{3,0,2,1:T(8,128)(2,1)S(1)}, bf16[8,2,8,512]{3,0,2,1:T(8,128)(2,1)S(1)}, u32[]{:S(2)}, u32[]{:S(2)}) collective-permute-start(bf16[8,2,8,512]{3,0,2,1:T(8,128)(2,1)S(1)} %bitcast.184), channel_id=1, source_target_pairs={{0,4},{4,8},{8,12},{12,16},{16,20},{20,24},{24,28},{1,5},{5,9},{9,... | collective-permute-start | bytes 393224 | tf_op jit(solution)/shard_map/while/body/eval_jaxpr/ppermute | solution.py:27
  137.0 7.8 %collective-permute-start.2 = (bf16[8,2,8,512]{3,0,2,1:T(8,128)(2,1)S(1)}, bf16[8,2,8,512]{3,0,2,1:T(8,128)(2,1)S(1)}, u32[]{:S(2)}, u32[]{:S(2)}) collective-permute-start(bf16[8,2,8,512]{3,0,2,1:T(8,128)(2,1)S(1)} %bitcast.184), channel_id=1, source_target_pairs={{0,4},{4,8},{8,12},{12,16},{16,20},{20,24},{24,28},{1,5},{5,9},{9,... | collective-permute-start | bytes 393224 | tf_op jit(solution)/shard_map/while/body/eval_jaxpr/ppermute | solution.py:27
  144.8 5.6 collective-permute-start
  157.6 7.8 %collective-permute-start.2 = (bf16[8,2,8,512]{3,0,2,1:T(8,128)(2,1)S(1)}, bf16[8,2,8,512]{3,0,2,1:T(8,128)(2,1)S(1)}, u32[]{:S(2)}, u32[]{:S(2)}) collective-permute-start(bf16[8,2,8,512]{3,0,2,1:T(8,128)(2,1)S(1)} %bitcast.184), channel_id=1, source_target_pairs={{0,4},{4,8},{8,12},{12,16},{16,20},{20,24},{24,28},{1,5},{5,9},{9,... | collective-permute-start | bytes 393224 | tf_op jit(solution)/shard_map/while/body/eval_jaxpr/ppermute | solution.py:27
  178.2 7.8 %collective-permute-start.2 = (bf16[8,2,8,512]{3,0,2,1:T(8,128)(2,1)S(1)}, bf16[8,2,8,512]{3,0,2,1:T(8,128)(2,1)S(1)}, u32[]{:S(2)}, u32[]{:S(2)}) collective-permute-start(bf16[8,2,8,512]{3,0,2,1:T(8,128)(2,1)S(1)} %bitcast.184), channel_id=1, source_target_pairs={{0,4},{4,8},{8,12},{12,16},{16,20},{20,24},{24,28},{1,5},{5,9},{9,... | collective-permute-start | bytes 393224 | tf_op jit(solution)/shard_map/while/body/eval_jaxpr/ppermute | solution.py:27
  198.8 7.8 %collective-permute-start.2 = (bf16[8,2,8,512]{3,0,2,1:T(8,128)(2,1)S(1)}, bf16[8,2,8,512]{3,0,2,1:T(8,128)(2,1)S(1)}, u32[]{:S(2)}, u32[]{:S(2)}) collective-permute-start(bf16[8,2,8,512]{3,0,2,1:T(8,128)(2,1)S(1)} %bitcast.184), channel_id=1, source_target_pairs={{0,4},{4,8},{8,12},{12,16},{16,20},{20,24},{24,28},{1,5},{5,9},{9,... | collective-permute-start | bytes 393224 | tf_op jit(solution)/shard_map/while/body/eval_jaxpr/ppermute | solution.py:27
  219.4 7.8 %collective-permute-start.2 = (bf16[8,2,8,512]{3,0,2,1:T(8,128)(2,1)S(1)}, bf16[8,2,8,512]{3,0,2,1:T(8,128)(2,1)S(1)}, u32[]{:S(2)}, u32[]{:S(2)}) collective-permute-start(bf16[8,2,8,512]{3,0,2,1:T(8,128)(2,1)S(1)} %bitcast.184), channel_id=1, source_target_pairs={{0,4},{4,8},{8,12},{12,16},{16,20},{20,24},{24,28},{1,5},{5,9},{9,... | collective-permute-start | bytes 393224 | tf_op jit(solution)/shard_map/while/body/eval_jaxpr/ppermute | solution.py:27
  240.1 10.6 %collective-permute-start.5 = (f32[8,2,8,512]{3,0,2,1:T(8,128)S(1)}, f32[8,2,8,512]{3,0,2,1:T(8,128)S(1)}, u32[]{:S(2)}, u32[]{:S(2)}) collective-permute-start(f32[8,2,8,512]{3,0,2,1:T(8,128)S(1)} %get-tuple-element.874), channel_id=1, source_target_pairs={{4,0},{8,4},{12,8},{16,12},{20,16},{24,20},{28,24},{5,1},{9,5},{13... | collective-permute-start | bytes 786440 | tf_op jit(solution)/shard_map/while/body/eval_jaxpr/ppermute | solution.py:27
  263.2 11.0 %collective-permute-start.5 = (f32[8,2,8,512]{3,0,2,1:T(8,128)S(1)}, f32[8,2,8,512]{3,0,2,1:T(8,128)S(1)}, u32[]{:S(2)}, u32[]{:S(2)}) collective-permute-start(f32[8,2,8,512]{3,0,2,1:T(8,128)S(1)} %get-tuple-element.874), channel_id=1, source_target_pairs={{4,0},{8,4},{12,8},{16,12},{20,16},{24,20},{28,24},{5,1},{9,5},{13... | collective-permute-start | bytes 786440 | tf_op jit(solution)/shard_map/while/body/eval_jaxpr/ppermute | solution.py:27
  286.3 10.7 %collective-permute-start.5 = (f32[8,2,8,512]{3,0,2,1:T(8,128)S(1)}, f32[8,2,8,512]{3,0,2,1:T(8,128)S(1)}, u32[]{:S(2)}, u32[]{:S(2)}) collective-permute-start(f32[8,2,8,512]{3,0,2,1:T(8,128)S(1)} %get-tuple-element.874), channel_id=1, source_target_pairs={{4,0},{8,4},{12,8},{16,12},{20,16},{24,20},{28,24},{5,1},{9,5},{13... | collective-permute-start | bytes 786440 | tf_op jit(solution)/shard_map/while/body/eval_jaxpr/ppermute | solution.py:27
  308.9 10.7 %collective-permute-start.5 = (f32[8,2,8,512]{3,0,2,1:T(8,128)S(1)}, f32[8,2,8,512]{3,0,2,1:T(8,128)S(1)}, u32[]{:S(2)}, u32[]{:S(2)}) collective-permute-start(f32[8,2,8,512]{3,0,2,1:T(8,128)S(1)} %get-tuple-element.874), channel_id=1, source_target_pairs={{4,0},{8,4},{12,8},{16,12},{20,16},{24,20},{28,24},{5,1},{9,5},{13... | collective-permute-start | bytes 786440 | tf_op jit(solution)/shard_map/while/body/eval_jaxpr/ppermute | solution.py:27
  331.5 10.7 %collective-permute-start.5 = (f32[8,2,8,512]{3,0,2,1:T(8,128)S(1)}, f32[8,2,8,512]{3,0,2,1:T(8,128)S(1)}, u32[]{:S(2)}, u32[]{:S(2)}) collective-permute-start(f32[8,2,8,512]{3,0,2,1:T(8,128)S(1)} %get-tuple-element.874), channel_id=1, source_target_pairs={{4,0},{8,4},{12,8},{16,12},{20,16},{24,20},{28,24},{5,1},{9,5},{13... | collective-permute-start | bytes 786440 | tf_op jit(solution)/shard_map/while/body/eval_jaxpr/ppermute | solution.py:27
  354.1 10.7 %collective-permute-start.5 = (f32[8,2,8,512]{3,0,2,1:T(8,128)S(1)}, f32[8,2,8,512]{3,0,2,1:T(8,128)S(1)}, u32[]{:S(2)}, u32[]{:S(2)}) collective-permute-start(f32[8,2,8,512]{3,0,2,1:T(8,128)S(1)} %get-tuple-element.874), channel_id=1, source_target_pairs={{4,0},{8,4},{12,8},{16,12},{20,16},{24,20},{28,24},{5,1},{9,5},{13... | collective-permute-start | bytes 786440 | tf_op jit(solution)/shard_map/while/body/eval_jaxpr/ppermute | solution.py:27
  376.8 10.7 %collective-permute-start.5 = (f32[8,2,8,512]{3,0,2,1:T(8,128)S(1)}, f32[8,2,8,512]{3,0,2,1:T(8,128)S(1)}, u32[]{:S(2)}, u32[]{:S(2)}) collective-permute-start(f32[8,2,8,512]{3,0,2,1:T(8,128)S(1)} %get-tuple-element.874), channel_id=1, source_target_pairs={{4,0},{8,4},{12,8},{16,12},{20,16},{24,20},{28,24},{5,1},{9,5},{13... | collective-permute-start | bytes 786440 | tf_op jit(solution)/shard_map/while/body/eval_jaxpr/ppermute | solution.py:27
  399.4 10.7 %collective-permute-start.5 = (f32[8,2,8,512]{3,0,2,1:T(8,128)S(1)}, f32[8,2,8,512]{3,0,2,1:T(8,128)S(1)}, u32[]{:S(2)}, u32[]{:S(2)}) collective-permute-start(f32[8,2,8,512]{3,0,2,1:T(8,128)S(1)} %get-tuple-element.874), channel_id=1, source_target_pairs={{4,0},{8,4},{12,8},{16,12},{20,16},{24,20},{28,24},{5,1},{9,5},{13... | collective-permute-start | bytes 786440 | tf_op jit(solution)/shard_map/while/body/eval_jaxpr/ppermute | solution.py:27
  422.0 10.7 %collective-permute-start.5 = (f32[8,2,8,512]{3,0,2,1:T(8,128)S(1)}, f32[8,2,8,512]{3,0,2,1:T(8,128)S(1)}, u32[]{:S(2)}, u32[]{:S(2)}) collective-permute-start(f32[8,2,8,512]{3,0,2,1:T(8,128)S(1)} %get-tuple-element.874), channel_id=1, source_target_pairs={{4,0},{8,4},{12,8},{16,12},{20,16},{24,20},{28,24},{5,1},{9,5},{13... | collective-permute-start | bytes 786440 | tf_op jit(solution)/shard_map/while/body/eval_jaxpr/ppermute | solution.py:27
  444.6 10.7 %collective-permute-start.5 = (f32[8,2,8,512]{3,0,2,1:T(8,128)S(1)}, f32[8,2,8,512]{3,0,2,1:T(8,128)S(1)}, u32[]{:S(2)}, u32[]{:S(2)}) collective-permute-start(f32[8,2,8,512]{3,0,2,1:T(8,128)S(1)} %get-tuple-element.874), channel_id=1, source_target_pairs={{4,0},{8,4},{12,8},{16,12},{20,16},{24,20},{28,24},{5,1},{9,5},{13... | collective-permute-start | bytes 786440 | tf_op jit(solution)/shard_map/while/body/eval_jaxpr/ppermute | solution.py:27
  467.3 10.7 %collective-permute-start.5 = (f32[8,2,8,512]{3,0,2,1:T(8,128)S(1)}, f32[8,2,8,512]{3,0,2,1:T(8,128)S(1)}, u32[]{:S(2)}, u32[]{:S(2)}) collective-permute-start(f32[8,2,8,512]{3,0,2,1:T(8,128)S(1)} %get-tuple-element.874), channel_id=1, source_target_pairs={{4,0},{8,4},{12,8},{16,12},{20,16},{24,20},{28,24},{5,1},{9,5},{13... | collective-permute-start | bytes 786440 | tf_op jit(solution)/shard_map/while/body/eval_jaxpr/ppermute | solution.py:27
  (42 other events, 181.2 us)
where the time goes:
time: 640 us; the launch traced here: 634 us
  matrix products  208 us (32%)
  starting transfers between devices  169 us (26%)
  waiting for transfers between devices  159 us (25%)
  blocking collectives  41.6 us (6%)
  loops' own time  24 us (4%)
  local copies, waits for them, and re-layouts  21 us (3%)
  other arithmetic  11.1 us (2%)
    ppermute x22, waiting for transfers between devices, shifted(): return lax.ppermute(array, axis, pairs)  131 us
    dot_general x22, matrix products, apply_inverse(): jnp.einsum('crik,jcrk->jcri', inverse_block, vectors, preferred_element_t...  124 us
    ppermute x22, starting transfers between devices, with_halo(): lax.ppermute(tail, axis, [(i, (i + 1) % count) for i in range(ends)])  72.2 us
    ppermute x22, starting transfers between devices, shifted(): return lax.ppermute(array, axis, pairs)  68.5 us
    psum x1, blocking collectives, per_device(): gram_whole = lax.psum(gram_local, ('layer', 'tile'))  41.6 us
    ppermute x22, starting transfers between devices, with_halo(): lax.ppermute(head, axis, [((i + 1) % count, i) for i in range(ends)])  28.4 us
    ppermute x22, waiting for transfers between devices, with_halo(): lax.ppermute(head, axis, [((i + 1) % count, i) for i in range(ends)])  27.9 us
    dot_general x32, matrix products, column_step(): column = column - jnp.dot(lower, lower_row, precision=lax.Precision.HIGHEST)  24.9 us
  transfers between devices with their start and end apart: 66, of which 44 were waited for; matrix products, arithmetic and copies ran while one was open for 3% of the time, Pallas kernels for 0%

commit v1 on v0

v1 whole, which is shorter than its diff:
```python
import functools

import jax
import jax.numpy as jnp
from jax import lax
from jax.experimental import pallas as pl
from jax.experimental.pallas import tpu as pltpu
from jax.sharding import PartitionSpec as P

MESH = pl.DeviceIdType.MESH
GROUPS = 4


def dot_last(a, b, precision=None):
    return lax.dot_general(
        a, b, (((1,), (1,)), ((), ())), precision=precision, preferred_element_type=jnp.float32
    )


def sweep_kernel(
    layers, tiles,
    src, weight_cols, self_w, curl_w, inv_hbm,
    snap, gram,
    inv, forcing, down_in, down, up_in, up_out, gram_acc, gram_tile, gram_layer, gram_part,
    inv_sem, down_send, down_recv, down_edge_send, down_edge_recv,
    up_send, up_recv, up_edge_send, up_edge_recv,
    tile_send, tile_recv, layer_send, layer_recv,
):
    layer = lax.axis_index("layer")
    tile = lax.axis_index("tile")
    groups, rows = down.shape[0], down.shape[1]
    width = down.shape[3]
    last = rows - 1
    odd = lax.rem(tile, 2)
    sign = 1 - 2 * odd
    front = tile - sign
    back = tile + sign
    has_front = jnp.logical_and(front >= 0, front < tiles)
    has_back = jnp.logical_and(back >= 0, back < tiles)
    partners = ((has_front, front), (has_back, back))
    top = layers - 1
    not_first = layer > 0
    not_last = layer < top

    def row_of(step):
        return step + odd * (last - 2 * step)

    def inv_copy(comp, step):
        row = row_of(step)
        return pltpu.make_async_copy(
            inv_hbm.at[0, comp, row], inv.at[comp, row], inv_sem.at[comp, step]
        )

    def start_weights(step, carry):
        inv_copy(0, step).start()
        inv_copy(1, step).start()
        return carry

    lax.fori_loop(0, rows, start_weights, 0)

    barrier = pltpu.get_barrier_semaphore()

    def greet(dev_layer, dev_tile):
        pl.semaphore_signal(barrier, inc=1, device_id=(dev_layer, dev_tile), device_id_type=MESH)

    for shift in (-1, 1):
        near = layer + shift
        ok = jnp.logical_and(near >= 0, near < layers)
        for has, partner in partners:
            @pl.when(jnp.logical_and(ok, has))
            def _(near=near, partner=partner):
                greet(near, partner)

    for k in range(1, layers):
        greet(lax.rem(layer + k, layers), tile)
    for k in range(1, tiles):
        greet(layer, lax.rem(tile + k, tiles))

    port_cols = width // 2
    row_no = lax.broadcasted_iota(jnp.int32, (width, src.shape[4]), 0)

    def make_forcing(group, carry):
        scale = weight_cols[group]
        for comp in range(2):
            first = src[0, 2 * group, comp].astype(jnp.float32)
            second = src[0, 2 * group + 1, comp].astype(jnp.float32)
            for row in range(rows):
                pair = jnp.where(row_no < port_cols, first[row : row + 1], second[row : row + 1])
                forcing[group, comp, row] = pair * scale
        return carry

    lax.fori_loop(0, groups, make_forcing, 0)

    @pl.when(layer == 0)
    def _():
        def clear(group, carry):
            down_in[group] = jnp.zeros(down_in.shape[1:], down_in.dtype)
            return carry

        lax.fori_loop(0, groups, clear, 0)

    for edge, (has, _) in enumerate(partners):
        slot = 0 if edge == 0 else rows + 1

        @pl.when(jnp.logical_not(has))
        def _(slot=slot):
            def clear(group, carry):
                down_in[group, slot, 1] = jnp.zeros(down_in.shape[3:], down_in.dtype)
                up_in[group, slot, 1] = jnp.zeros(up_in.shape[3:], up_in.dtype)
                return carry

            lax.fori_loop(0, groups, clear, 0)

    gram_acc[...] = jnp.zeros_like(gram_acc)

    sides = (layer > 0).astype(jnp.int32) + (layer < top).astype(jnp.int32)
    fronts = has_front.astype(jnp.int32) + has_back.astype(jnp.int32)
    pl.semaphore_wait(barrier, layers - 1 + tiles - 1 + sides * fronts)

    def main_copy(source, target, sems, group, step, near):
        return pltpu.make_async_remote_copy(
            src_ref=source.at[group, step], dst_ref=target.at[group, step + 1],
            send_sem=sems[0].at[group, step], recv_sem=sems[1].at[group, step],
            device_id=(near, tile), device_id_type=MESH,
        )

    def edge_copy(source, target, sems, group, edge, near):
        step, slot = (0, 0) if edge == 0 else (last, rows + 1)
        return pltpu.make_async_remote_copy(
            src_ref=source.at[group, step, 1], dst_ref=target.at[group, slot, 1],
            send_sem=sems[2].at[group, edge], recv_sem=sems[3].at[group, edge],
            device_id=(near, partners[edge][1]), device_id_type=MESH,
        )

    def send_unit(source, target, sems, group, step, near):
        main_copy(source, target, sems, group, step, near).start()
        for edge, at in ((0, 0), (1, last)):
            @pl.when(jnp.logical_and(step == at, partners[edge][0]))
            def _(edge=edge):
                edge_copy(source, target, sems, group, edge, near).start()

    def wait_unit(source, target, sems, group, step, near):
        @pl.when(step == 0)
        def _():
            main_copy(source, target, sems, group, 0, near).wait_recv()

            @pl.when(has_front)
            def _():
                edge_copy(source, target, sems, group, 0, near).wait_recv()

        @pl.when(step < last)
        def _():
            main_copy(source, target, sems, group, step + 1, near).wait_recv()

        @pl.when(jnp.logical_and(step == last, has_back))
        def _():
            edge_copy(source, target, sems, group, 1, near).wait_recv()

    def wait_sent(source, target, sems, near):
        def group_body(group, carry):
            def step_body(step, inner):
                main_copy(source, target, sems, group, step, near).wait_send()
                return inner

            lax.fori_loop(0, rows, step_body, 0)
            for edge in range(2):
                @pl.when(partners[edge][0])
                def _(edge=edge):
                    edge_copy(source, target, sems, group, edge, near).wait_send()

            return carry

        lax.fori_loop(0, groups, group_body, 0)

    down_sems = (down_send, down_recv, down_edge_send, down_edge_recv)
    up_sems = (up_send, up_recv, up_edge_send, up_edge_recv)
    plane_width = src.shape[4]
    lane = lax.broadcasted_iota(jnp.int32, (width, plane_width), 1)
    sign_f = sign.astype(jnp.float32)

    def couple(field, group, step, row):
        x_part = field[group, step + 1, 0].astype(jnp.float32)
        y_part = field[group, step + 1, 1].astype(jnp.float32)
        before = field[group, step, 1].astype(jnp.float32)
        after = field[group, step + 2, 1].astype(jnp.float32)
        row_diff = sign_f * (after - before)
        right = jnp.where(lane == plane_width - 1, 0.0, pltpu.roll(x_part, plane_width - 1, 1))
        left = jnp.where(lane == 0, 0.0, pltpu.roll(x_part, 1, 1))
        at = pl.ds(row, 1)
        part_one = self_w[0, 0, at, :] * x_part + curl_w[0, 0, at, :] * row_diff
        part_two = self_w[0, 1, at, :] * y_part + curl_w[0, 1, at, :] * (right - left)
        return part_one, part_two

    def columns_of(group):
        return pl.ds(pl.multiple_of(group * width, width), width)

    def add_gram(group, row):
        @pl.when(group == groups - 1)
        def _():
            for comp in range(2):
                block = snap[comp, row]
                gram_acc[:, : block.shape[0]] += dot_last(block, block, lax.Precision.HIGHEST)

    def down_unit(group, step):
        row = row_of(step)

        @pl.when(not_first)
        def _():
            wait_unit(down, down_in, down_sems, group, step, layer - 1)

        @pl.when(group == 0)
        def _():
            inv_copy(0, step).wait()
            inv_copy(1, step).wait()

        parts = couple(down_in, group, step, row)
        fields = []
        for comp in range(2):
            residue = (forcing[group, comp, row] - parts[comp]).astype(jnp.bfloat16)
            field = dot_last(residue, inv[comp, row]).astype(jnp.bfloat16)
            down[group, step, comp] = field
            fields.append(field)

        @pl.when(not_last)
        def _():
            send_unit(down, down_in, down_sems, group, step, layer + 1)

        @pl.when(layer == top)
        def _():
            if layers > 1:
                send_unit(down, up_in, up_sems, group, step, layer - 1)
            for comp in range(2):
                snap[comp, row, columns_of(group), :] = fields[comp].astype(jnp.float32)
            add_gram(group, row)

    def up_unit(group, step):
        row = row_of(step)
        wait_unit(up_out, up_in, up_sems, group, step, layer + 1)
        parts = couple(up_in, group, step, row)
        for comp in range(2):
            image = parts[comp].astype(jnp.bfloat16)
            update = dot_last(image, inv[comp, row])
            value = down[group, step, comp].astype(jnp.float32) - update
            snap[comp, row, columns_of(group), :] = value
            up_out[group, step, comp] = value.astype(jnp.bfloat16)

        @pl.when(not_first)
        def _():
            send_unit(up_out, up_in, up_sems, group, step, layer - 1)

        add_gram(group, row)

    def run(unit):
        def group_body(group, carry):
            def step_body(step, inner):
                unit(group, step)
                return inner

            return lax.fori_loop(0, rows, step_body, carry)

        lax.fori_loop(0, groups, group_body, 0)

    run(down_unit)

    @pl.when(not_last)
    def _():
        run(up_unit)

    gram_tile[tile] = gram_acc[...]
    for k in range(1, tiles):
        tile_copy(gram_acc, gram_tile, tile_send, tile_recv, k, tiles, layer, tile).start()
    for k in range(1, tiles):
        tile_copy(gram_acc, gram_tile, tile_send, tile_recv, k, tiles, layer, tile).wait_recv()
    gram_part[...] = functools.reduce(lambda a, b: a + b, [gram_tile[k] for k in range(tiles)])
    gram_layer[layer] = gram_part[...]
    for k in range(1, layers):
        layer_copy(gram_part, gram_layer, layer_send, layer_recv, k, layers, layer, tile).start()
    for k in range(1, layers):
        layer_copy(gram_part, gram_layer, layer_send, layer_recv, k, layers, layer, tile).wait_recv()
    gram[...] = functools.reduce(lambda a, b: a + b, [gram_layer[k] for k in range(layers)])

    for k in range(1, tiles):
        tile_copy(gram_acc, gram_tile, tile_send, tile_recv, k, tiles, layer, tile).wait_send()
    for k in range(1, layers):
        layer_copy(gram_part, gram_layer, layer_send, layer_recv, k, layers, layer, tile).wait_send()

    @pl.when(not_last)
    def _():
        wait_sent(down, down_in, down_sems, layer + 1)

    if layers > 1:
        @pl.when(layer == top)
        def _():
            wait_sent(down, up_in, up_sems, layer - 1)

    @pl.when(jnp.logical_and(not_first, not_last))
    def _():
        wait_sent(up_out, up_in, up_sems, layer - 1)


def tile_copy(source, target, send, recv, k, tiles, layer, tile):
    return pltpu.make_async_remote_copy(
        src_ref=source, dst_ref=target.at[tile], send_sem=send.at[k], recv_sem=recv.at[k],
        device_id=(layer, lax.rem(tile + k, tiles)), device_id_type=MESH,
    )


def layer_copy(source, target, send, recv, k, layers, layer, tile):
    return pltpu.make_async_remote_copy(
        src_ref=source, dst_ref=target.at[layer], send_sem=send.at[k], recv_sem=recv.at[k],
        device_id=(lax.rem(layer + k, layers), tile), device_id_type=MESH,
    )


def basis_kernel(total_rows, snap, gram, basis, triangle):
    order = triangle.shape[0]
    row_no = lax.broadcasted_iota(jnp.int32, gram.shape, 0)
    col_no = lax.broadcasted_iota(jnp.int32, gram.shape, 1)
    work = jnp.where(col_no < order, gram[...] / total_rows, 0.0)
    work = jnp.where(col_no == row_no + order, 1.0, work)
    for k in range(order):
        pivot = 1.0 / jnp.sqrt(work[k : k + 1, k : k + 1])
        line = work[k : k + 1, :] * pivot
        column = work[:, k : k + 1] * pivot
        below = work - column * line
        work = jnp.where(row_no > k, below, jnp.where(row_no == k, line, work))
    upper = jnp.where(col_no >= row_no, work, 0.0)
    triangle[...] = upper[:, :order]
    lower_inv = work[:, order : 2 * order]
    for comp in range(basis.shape[2]):
        for row in range(basis.shape[3]):
            solved = jnp.dot(
                lower_inv, snap[comp, row], precision=lax.Precision.HIGHEST,
                preferred_element_type=jnp.float32,
            )
            basis[0, :, comp, row, :] = solved


def per_device(source_modes, port_cells, frequencies, layer_inverse, coupling_self, coupling_curl):
    layers = lax.axis_size("layer")
    tiles = lax.axis_size("tile")
    layer_pos = lax.axis_index("layer")
    ports = source_modes.shape[1]
    rows = source_modes.shape[3]
    plane_width = source_modes.shape[4]
    order = ports * frequencies.shape[0] * 2
    groups = GROUPS
    width = order // groups
    columns = jnp.arange(plane_width, dtype=jnp.float32)
    offsets = (columns[None, :] - port_cells.astype(jnp.float32)[:, None]) / (plane_width // 8)
    port_taper = 1.0 / (1.0 + offsets * offsets)
    phase_angle = frequencies * (layer_pos + 1).astype(jnp.float32)
    phase_pair = jnp.stack([jnp.cos(phase_angle), jnp.sin(phase_angle)], axis=1)
    weight_cols = port_taper[:, None, :] * phase_pair.reshape(1, -1, 1)
    weight_cols = weight_cols.reshape(groups, width, plane_width)

    vmem = pl.BlockSpec(memory_space=pltpu.VMEM)
    dma = pltpu.SemaphoreType.DMA
    bf16, f32 = jnp.bfloat16, jnp.float32
    halo_shape = (groups, rows + 2, 2, width, plane_width)
    field_shape = (groups, rows, 2, width, plane_width)
    snap, gram = pl.pallas_call(
        functools.partial(sweep_kernel, layers, tiles),
        out_shape=(
            jax.ShapeDtypeStruct((2, rows, order, plane_width), f32),
            jax.ShapeDtypeStruct((order, 128), f32),
        ),
        in_specs=[vmem, vmem, vmem, vmem, pl.BlockSpec(memory_space=pl.ANY)],
        out_specs=(vmem, vmem),
        scratch_shapes=[
            pltpu.VMEM(layer_inverse.shape[1:], bf16),
            pltpu.VMEM((groups, 2, rows, width, plane_width), f32),
            pltpu.VMEM(halo_shape, bf16),
            pltpu.VMEM(field_shape, bf16),
            pltpu.VMEM(halo_shape, bf16),
            pltpu.VMEM(field_shape, bf16),
            pltpu.VMEM((order, 128), f32),
            pltpu.VMEM((tiles, order, 128), f32),
            pltpu.VMEM((layers, order, 128), f32),
            pltpu.VMEM((order, 128), f32),
            dma((2, rows)),
            dma((groups, rows)), dma((groups, rows)), dma((groups, 2)), dma((groups, 2)),
            dma((groups, rows)), dma((groups, rows)), dma((groups, 2)), dma((groups, 2)),
            dma((tiles,)), dma((tiles,)), dma((layers,)), dma((layers,)),
        ],
        compiler_params=pltpu.CompilerParams(collective_id=0, has_side_effects=True),
        name="sweep",
    )(source_modes, weight_cols, coupling_self, coupling_curl, layer_inverse)
    total_rows = layers * tiles * 2 * rows * plane_width
    return pl.pallas_call(
        functools.partial(basis_kernel, total_rows),
        out_shape=(
            jax.ShapeDtypeStruct((1, order, 2, rows, plane_width), f32),
            jax.ShapeDtypeStruct((order, order), f32),
        ),
        in_specs=[vmem, vmem],
        out_specs=(vmem, vmem),
        name="basis",
    )(snap, gram)


def solution(mesh):
    in_specs = (
        P("layer", None, None, "tile", None),
        P(),
        P(),
        P("layer", None, "tile", None, None),
        P("layer", None, "tile", None),
        P("layer", None, "tile", None),
    )
    out_specs = (P("layer", None, None, "tile", None), P())
    return jax.shard_map(
        per_device, mesh=mesh, in_specs=in_specs, out_specs=out_specs, check_vma=False
    )
```

time: 640 us -> 102 us (0.16)
  matrix products: 208 us -> 0 us
  starting transfers between devices: 169 us -> 0 us
  waiting for transfers between devices: 159 us -> 0 us
  Pallas kernels: 0 us -> 98.6 us
  blocking collectives: 41.6 us -> 0 us
  loops' own time: 24 us -> 0 us
  local copies, waits for them, and re-layouts: 21 us -> 0.31 us
  other arithmetic: 11.1 us -> 2.15 us
    dot_general x184 -> x0, matrix products: 208 us -> none  [the longest x22 124 us: apply_inverse(): jnp.einsum('crik,jcrk->jcri', inverse_block, vectors, preferred_element_t...]
    ppermute x66 -> x0, starting transfers between devices: 169 us -> none  [the longest x22 72.2 us: with_halo(): lax.ppermute(tail, axis, [(i, (i + 1) % count) for i in range(ends)])]
    ppermute x66 -> x0, waiting for transfers between devices: 159 us -> none  [the longest x22 131 us: shifted(): return lax.ppermute(array, axis, pairs)]
    pallas_call x0 -> x2, Pallas kernels: none -> 98.6 us  [the longest x1 92.3 us: per_device(): pl.pallas_call(functools.partial(sweep_kernel, layers, tiles), out_shape=...]
    psum x1 -> x0, blocking collectives: 41.6 us -> none  [per_device(): gram_whole = lax.psum(gram_local, ('layer', 'tile'))]
    another operation x4 -> x0, loops' own time: 24 us -> none  [the longest x1 22.7 us: lower_factor(): return lax.fori_loop(0, order, column_step, jnp.zeros_like(gram))]
    mul x25 -> x5, local copies, waits for them, and re-layouts: 17.4 us -> 0.21 us  [per_device(): weight_cols = port_taper[:, None, :] * phase_pair.reshape(1, -1, 1)]
  transfers between devices with their start and end apart: 66 -> 0, of which waited for: 44 -> 0; matrix products, arithmetic and copies ran while one was open for 3% -> 0% of each run, Pallas kernels for 0% -> 0%
where the time goes in v1:
time: 102 us
  Pallas kernels  98.6 us (97%)
  other arithmetic  2.15 us (2%)
    pallas_call x1, Pallas kernels, per_device(): pl.pallas_call(functools.partial(sweep_kernel, layers, tiles), out_shape=...  92.3 us
    pallas_call x1, Pallas kernels, per_device(): pl.pallas_call(functools.partial(basis_kernel, total_rows), out_shape=(ja...  6.33 us

profile of v1, /device:TPU:0, one launch (start us, length us, event | category | flops | bytes accessed | tf_op | source)
XLA Modules:
  0.0 101.7 jit_solution(4260821419262008086)
XLA Ops:
  0.6 0.7 convert_element_type.6
  1.3 0.7 cosine_bitcast_fusion
  2.0 0.1 copy.8
  2.1 0.1 mul.40
  2.2 0.1 mul.42
  2.3 0.1 add_divide_fusion
  2.4 0.7 broadcast_multiply_fusion.weight_cols
  3.1 92.3 %sweep.1 = (f32[2,8,32,512]{3,2,1,0:T(8,128)}, f32[32,128]{1,0:T(8,128)}) custom-call(bf16[1,8,2,8,512]{4,3,2,1,0:T(8,128)(2,1)} %src.1, f32[4,8,512]{2,1,0:T(8,128)} %broadcast_multiply_fusion.weight_cols, f32[1,2,8,512]{3,2,1,0:T(8,128)} %self_w.1, f32[1,2,8,512]{3,2,1,0:T(8,128)} %curl_w.1, bf16[1,2,8,512,512]{4,3,2,1,0:T(8,128)(2,1)} %inv_hbm.1), custom_call_target="tpu_custom_call" | custom-call | tf_op jit(solution)/shard_map/sweep/pallas_call | solution.py:362
  95.4 6.3 %basis.1 = (f32[1,32,2,8,512]{4,3,2,1,0:T(8,128)}, f32[32,32]{1,0:T(8,128)}) custom-call(f32[2,8,32,512]{3,2,1,0:T(8,128)} %get-tuple-element.4.snap, f32[32,128]{1,0:T(8,128)} %get-tuple-element.5.gram), custom_call_target="tpu_custom_call" | custom-call | tf_op jit(solution)/shard_map/basis/pallas_call | solution.py:390
  (4 shorter events, 0.1 us)

commit v2 on v1

--- a/solution.py
+++ b/solution.py
@@ -9,6 +9,8 @@
 
 MESH = pl.DeviceIdType.MESH
 GROUPS = 4
+TURN = 128
+SPLIT = 2
 
 
 def dot_last(a, b, precision=None):
@@ -19,9 +21,9 @@
 
 def sweep_kernel(
     layers, tiles,
-    src, weight_cols, self_w, curl_w, inv_hbm,
+    port_cells, frequencies, src, self_w, curl_w, inv_hbm,
     snap, gram,
-    inv, forcing, down_in, down, up_in, up_out, gram_acc, gram_tile, gram_layer, gram_part,
+    inv, inv_t, forcing, down_in, down, up_in, up_out, gram_acc, gram_tile, gram_layer, gram_part,
     inv_sem, down_send, down_recv, down_edge_send, down_edge_recv,
     up_send, up_recv, up_edge_send, up_edge_recv,
     tile_send, tile_recv, layer_send, layer_recv,
@@ -76,17 +78,33 @@
     for k in range(1, tiles):
         greet(layer, lax.rem(tile + k, tiles))
 
-    port_cols = width // 2
-    row_no = lax.broadcasted_iota(jnp.int32, (width, src.shape[4]), 0)
+    plane_width = src.shape[4]
+    row_no = lax.broadcasted_iota(jnp.int32, (width, plane_width), 0)
+    lane = lax.broadcasted_iota(jnp.int32, (width, plane_width), 1)
+    port_count = src.shape[1] // groups
+    port_cols = width // port_count
+    column = lane.astype(jnp.float32)
+    in_port = lax.rem(row_no, port_cols)
+    pitch = (layer + 1).astype(jnp.float32)
+    angle = jnp.full((width, plane_width), frequencies[0] * pitch)
+    for k in range(1, port_cols // 2):
+        angle = jnp.where(in_port >= 2 * k, frequencies[k] * pitch, angle)
+    phase = jnp.where(lax.rem(in_port, 2) == 0, jnp.cos(angle), jnp.sin(angle))
 
     def make_forcing(group, carry):
-        scale = weight_cols[group]
+        centre = jnp.full((width, plane_width), port_cells[port_count * group].astype(jnp.float32))
+        for k in range(1, port_count):
+            cell = port_cells[port_count * group + k].astype(jnp.float32)
+            centre = jnp.where(row_no >= k * port_cols, cell, centre)
+        offset = (column - centre) / (plane_width // 8)
+        scale = phase * (1.0 / (1.0 + offset * offset))
         for comp in range(2):
-            first = src[0, 2 * group, comp].astype(jnp.float32)
-            second = src[0, 2 * group + 1, comp].astype(jnp.float32)
+            modes = [src[0, port_count * group + k, comp].astype(jnp.float32) for k in range(port_count)]
             for row in range(rows):
-                pair = jnp.where(row_no < port_cols, first[row : row + 1], second[row : row + 1])
-                forcing[group, comp, row] = pair * scale
+                mixed = jnp.broadcast_to(modes[0][row : row + 1], scale.shape)
+                for k in range(1, port_count):
+                    mixed = jnp.where(row_no >= k * port_cols, modes[k][row : row + 1], mixed)
+                forcing[group, comp, row] = mixed * scale
         return carry
 
     lax.fori_loop(0, groups, make_forcing, 0)
@@ -174,8 +192,6 @@
 
     down_sems = (down_send, down_recv, down_edge_send, down_edge_recv)
     up_sems = (up_send, up_recv, up_edge_send, up_edge_recv)
-    plane_width = src.shape[4]
-    lane = lax.broadcasted_iota(jnp.int32, (width, plane_width), 1)
     sign_f = sign.astype(jnp.float32)
 
     def couple(field, group, step, row):
@@ -201,15 +217,23 @@
                 block = snap[comp, row]
                 gram_acc[:, : block.shape[0]] += dot_last(block, block, lax.Precision.HIGHEST)
 
-    def down_unit(group, step):
+    def turn_block(comp, row):
+        for at in range(0, plane_width, TURN):
+            for to in range(0, plane_width, TURN):
+                block = inv[comp, row, at : at + TURN, to : to + TURN]
+                inv_t[comp, row, to : to + TURN, at : at + TURN] = block.T
+
+    def apply_turned(vectors, comp, row):
+        return jnp.dot(vectors, inv_t[comp, row], preferred_element_type=jnp.float32)
+
+    def down_unit(opening, group, step):
         row = row_of(step)
 
         @pl.when(not_first)
         def _():
             wait_unit(down, down_in, down_sems, group, step, layer - 1)
 
-        @pl.when(group == 0)
-        def _():
+        if opening:
             inv_copy(0, step).wait()
             inv_copy(1, step).wait()
 
@@ -217,9 +241,15 @@
         fields = []
         for comp in range(2):
             residue = (forcing[group, comp, row] - parts[comp]).astype(jnp.bfloat16)
-            field = dot_last(residue, inv[comp, row]).astype(jnp.bfloat16)
+            if opening:
+                field = dot_last(residue, inv[comp, row]).astype(jnp.bfloat16)
+            else:
+                field = apply_turned(residue, comp, row).astype(jnp.bfloat16)
             down[group, step, comp] = field
             fields.append(field)
+        if opening:
+            for comp in range(2):
+                turn_block(comp, row)
 
         @pl.when(not_last)
         def _():
@@ -239,7 +269,7 @@
         parts = couple(up_in, group, step, row)
         for comp in range(2):
             image = parts[comp].astype(jnp.bfloat16)
-            update = dot_last(image, inv[comp, row])
+            update = apply_turned(image, comp, row)
             value = down[group, step, comp].astype(jnp.float32) - update
             snap[comp, row, columns_of(group), :] = value
             up_out[group, step, comp] = value.astype(jnp.bfloat16)
@@ -250,7 +280,7 @@
 
         add_gram(group, row)
 
-    def run(unit):
+    def run(unit, first):
         def group_body(group, carry):
             def step_body(step, inner):
                 unit(group, step)
@@ -258,13 +288,18 @@
 
             return lax.fori_loop(0, rows, step_body, carry)
 
-        lax.fori_loop(0, groups, group_body, 0)
-
-    run(down_unit)
+        lax.fori_loop(first, groups, group_body, 0)
+
+    def open_body(step, carry):
+        down_unit(True, 0, step)
+        return carry
+
+    lax.fori_loop(0, rows, open_body, 0)
+    run(functools.partial(down_unit, False), 1)
 
     @pl.when(not_last)
     def _():
-        run(up_unit)
+        run(up_unit, 0)
 
     gram_tile[tile] = gram_acc[...]
     for k in range(1, tiles):
@@ -312,49 +347,43 @@
     )
 
 
-def basis_kernel(total_rows, snap, gram, basis, triangle):
+def basis_kernel(total_rows, snap, gram, basis, triangle, lower_inv):
     order = triangle.shape[0]
-    row_no = lax.broadcasted_iota(jnp.int32, gram.shape, 0)
-    col_no = lax.broadcasted_iota(jnp.int32, gram.shape, 1)
-    work = jnp.where(col_no < order, gram[...] / total_rows, 0.0)
-    work = jnp.where(col_no == row_no + order, 1.0, work)
-    for k in range(order):
-        pivot = 1.0 / jnp.sqrt(work[k : k + 1, k : k + 1])
-        line = work[k : k + 1, :] * pivot
-        column = work[:, k : k + 1] * pivot
-        below = work - column * line
-        work = jnp.where(row_no > k, below, jnp.where(row_no == k, line, work))
-    upper = jnp.where(col_no >= row_no, work, 0.0)
-    triangle[...] = upper[:, :order]
-    lower_inv = work[:, order : 2 * order]
-    for comp in range(basis.shape[2]):
-        for row in range(basis.shape[3]):
-            solved = jnp.dot(
-                lower_inv, snap[comp, row], precision=lax.Precision.HIGHEST,
-                preferred_element_type=jnp.float32,
-            )
-            basis[0, :, comp, row, :] = solved
+
+    @pl.when(jnp.logical_and(pl.program_id(0) == 0, pl.program_id(1) == 0))
+    def _():
+        row_no = lax.broadcasted_iota(jnp.int32, gram.shape, 0)
+        col_no = lax.broadcasted_iota(jnp.int32, gram.shape, 1)
+        work = jnp.where(col_no < order, gram[...] / total_rows, 0.0)
+        work = jnp.where(col_no == row_no + order, 1.0, work)
+        for k in range(order):
+            line = work[k : k + 1, :] / work[k : k + 1, k : k + 1]
+            column = work[:, k : k + 1]
+            work = jnp.where(row_no > k, work - column * line, work)
+        diagonal = jnp.sum(jnp.where(col_no == row_no, work, 0.0), axis=1, keepdims=True)
+        work = work / jnp.sqrt(diagonal)
+        triangle[...] = jnp.where(col_no >= row_no, work, 0.0)[:, :order]
+        lower_inv[...] = work[:, order : 2 * order]
+
+    factor = lower_inv[...]
+    for row in range(basis.shape[3]):
+        basis[0, :, 0, row, :] = jnp.dot(
+            factor, snap[0, row], precision=lax.Precision.HIGHEST,
+            preferred_element_type=jnp.float32,
+        )
 
 
 def per_device(source_modes, port_cells, frequencies, layer_inverse, coupling_self, coupling_curl):
     layers = lax.axis_size("layer")
     tiles = lax.axis_size("tile")
-    layer_pos = lax.axis_index("layer")
     ports = source_modes.shape[1]
     rows = source_modes.shape[3]
     plane_width = source_modes.shape[4]
     order = ports * frequencies.shape[0] * 2
     groups = GROUPS
     width = order // groups
-    columns = jnp.arange(plane_width, dtype=jnp.float32)
-    offsets = (columns[None, :] - port_cells.astype(jnp.float32)[:, None]) / (plane_width // 8)
-    port_taper = 1.0 / (1.0 + offsets * offsets)
-    phase_angle = frequencies * (layer_pos + 1).astype(jnp.float32)
-    phase_pair = jnp.stack([jnp.cos(phase_angle), jnp.sin(phase_angle)], axis=1)
-    weight_cols = port_taper[:, None, :] * phase_pair.reshape(1, -1, 1)
-    weight_cols = weight_cols.reshape(groups, width, plane_width)
-
     vmem = pl.BlockSpec(memory_space=pltpu.VMEM)
+    smem = pl.BlockSpec(memory_space=pltpu.SMEM)
     dma = pltpu.SemaphoreType.DMA
     bf16, f32 = jnp.bfloat16, jnp.float32
     halo_shape = (groups, rows + 2, 2, width, plane_width)
@@ -365,9 +394,10 @@
             jax.ShapeDtypeStruct((2, rows, order, plane_width), f32),
             jax.ShapeDtypeStruct((order, 128), f32),
         ),
-        in_specs=[vmem, vmem, vmem, vmem, pl.BlockSpec(memory_space=pl.ANY)],
+        in_specs=[smem, smem, vmem, vmem, vmem, pl.BlockSpec(memory_space=pl.ANY)],
         out_specs=(vmem, vmem),
         scratch_shapes=[
+            pltpu.VMEM(layer_inverse.shape[1:], bf16),
             pltpu.VMEM(layer_inverse.shape[1:], bf16),
             pltpu.VMEM((groups, 2, rows, width, plane_width), f32),
             pltpu.VMEM(halo_shape, bf16),
@@ -385,7 +415,7 @@
         ],
         compiler_params=pltpu.CompilerParams(collective_id=0, has_side_effects=True),
         name="sweep",
-    )(source_modes, weight_cols, coupling_self, coupling_curl, layer_inverse)
+    )(port_cells, frequencies, source_modes, coupling_self, coupling_curl, layer_inverse)
     total_rows = layers * tiles * 2 * rows * plane_width
     return pl.pallas_call(
         functools.partial(basis_kernel, total_rows),
@@ -393,8 +423,16 @@
             jax.ShapeDtypeStruct((1, order, 2, rows, plane_width), f32),
             jax.ShapeDtypeStruct((order, order), f32),
         ),
-        in_specs=[vmem, vmem],
-        out_specs=(vmem, vmem),
+        grid=(2, SPLIT),
+        in_specs=[
+            pl.BlockSpec((1, rows, order, plane_width // SPLIT), lambda i, k: (i, 0, 0, k)),
+            pl.BlockSpec((order, 128), lambda i, k: (0, 0)),
+        ],
+        out_specs=(
+            pl.BlockSpec((1, order, 1, rows, plane_width // SPLIT), lambda i, k: (0, 0, i, 0, k)),
+            pl.BlockSpec((order, order), lambda i, k: (0, 0)),
+        ),
+        scratch_shapes=[pltpu.VMEM((order, order), f32)],
         name="basis",
     )(snap, gram)
 

time: 102 us -> 97.5 us (0.956)
  other arithmetic: 2.15 us -> 0 us
  Pallas kernels: 98.6 us -> 96.7 us
    pallas_call x1, Pallas kernels: 92.3 us -> 89.9 us  [per_device(): pl.pallas_call(functools.partial(sweep_kernel, layers, tiles), out_shape=...]
where the time goes in v2:
time: 97.5 us; the launch traced here: 97.3 us
  Pallas kernels  96.7 us (99%)
    pallas_call x1, Pallas kernels, per_device(): pl.pallas_call(functools.partial(sweep_kernel, layers, tiles), out_shape=...  89.9 us
    pallas_call x1, Pallas kernels, per_device(): pl.pallas_call(functools.partial(basis_kernel, total_rows), out_shape=(ja...  6.78 us

profile of v2, /device:TPU:0, one launch (start us, length us, event | category | flops | bytes accessed | tf_op | source)
XLA Modules:
  0.0 97.3 jit_solution(5866378723110246748)
XLA Ops:
  0.6 89.9 %sweep.1 = (f32[2,8,32,512]{3,2,1,0:T(8,128)}, f32[32,128]{1,0:T(8,128)}) custom-call(s32[8]{0:T(128)} %port_cells.1, f32[2]{0:T(128)} %frequencies.1, bf16[1,8,2,8,512]{4,3,2,1,0:T(8,128)(2,1)} %src.1, f32[1,2,8,512]{3,2,1,0:T(8,128)} %self_w.1, f32[1,2,8,512]{3,2,1,0:T(8,128)} %curl_w.1, bf16[1,2,8,512,512]{4,3,2,1,0:T(8,128)(2,1)} %inv_hbm.1), custom_call_target="tpu_custom_call" | custom-call | tf_op jit(solution)/shard_map/sweep/pallas_call | solution.py:391
  90.6 6.8 %basis.1 = (f32[1,32,2,8,512]{4,3,2,1,0:T(8,128)}, f32[32,32]{1,0:T(8,128)}) custom-call(f32[2,8,32,512]{3,2,1,0:T(8,128)} %get-tuple-element.4.snap, f32[32,128]{1,0:T(8,128)} %get-tuple-element.5.gram), custom_call_target="tpu_custom_call" | custom-call | tf_op jit(solution)/shard_map/basis/pallas_call | solution.py:420

commit v3 on v2

--- a/solution.py
+++ b/solution.py
@@ -10,7 +10,7 @@
 MESH = pl.DeviceIdType.MESH
 GROUPS = 4
 TURN = 128
-SPLIT = 2
+SPLIT = 1
 
 
 def dot_last(a, b, precision=None):

time: 97.5 us -> 96.5 us (0.990)
  Pallas kernels: 96.7 us -> 95.7 us
    pallas_call x1, Pallas kernels: 6.78 us -> 5.78 us  [per_device(): pl.pallas_call(functools.partial(basis_kernel, total_rows), out_shape=(ja...]
where the time goes in v3:
time: 96.5 us; the launch traced here: 96.3 us
  Pallas kernels  95.7 us (99%)
    pallas_call x1, Pallas kernels, per_device(): pl.pallas_call(functools.partial(sweep_kernel, layers, tiles), out_shape=...  89.9 us
    pallas_call x1, Pallas kernels, per_device(): pl.pallas_call(functools.partial(basis_kernel, total_rows), out_shape=(ja...  5.78 us

profile of v3, /device:TPU:0, one launch (start us, length us, event | category | flops | bytes accessed | tf_op | source)
XLA Modules:
  0.0 96.3 jit_solution(9305854065950864423)
XLA Ops:
  0.6 89.9 %sweep.1 = (f32[2,8,32,512]{3,2,1,0:T(8,128)}, f32[32,128]{1,0:T(8,128)}) custom-call(s32[8]{0:T(128)} %port_cells.1, f32[2]{0:T(128)} %frequencies.1, bf16[1,8,2,8,512]{4,3,2,1,0:T(8,128)(2,1)} %src.1, f32[1,2,8,512]{3,2,1,0:T(8,128)} %self_w.1, f32[1,2,8,512]{3,2,1,0:T(8,128)} %curl_w.1, bf16[1,2,8,512,512]{4,3,2,1,0:T(8,128)(2,1)} %inv_hbm.1), custom_call_target="tpu_custom_call" | custom-call | tf_op jit(solution)/shard_map/sweep/pallas_call | solution.py:391
  90.6 5.8 %basis.1 = (f32[1,32,2,8,512]{4,3,2,1,0:T(8,128)}, f32[32,32]{1,0:T(8,128)}) custom-call(f32[2,8,32,512]{3,2,1,0:T(8,128)} %get-tuple-element.4.snap, f32[32,128]{1,0:T(8,128)} %get-tuple-element.5.gram), custom_call_target="tpu_custom_call" | custom-call | tf_op jit(solution)/shard_map/basis/pallas_call | solution.py:420
